TPU v7x, 256 devices: a whole 4x4x8 slice. The times are simulated.
256 devices in a mesh: tiles: 32 (over z, x), sub: 8 (over y, core).
Axes of the slice: x: 4, y: 4, z: 8, core: 2. Of those that a mesh axis runs over, the one named last changes fastest.
Arguments:
- latents: float32 [196608, 512], P(('tiles', 'sub')), may hold values from -130 to 130
- conv_weight: float32 [512, 9, 512], P('tiles'), may hold values from -0.09375 to 0.09375
- conv_bias: float32 [512], replicated, may hold values from -4 to 4
- norm1_gain: float32 [512], replicated, may hold values from 0.5 to 1.5
- norm1_shift: float32 [512], replicated, may hold values from -3 to 3
- norm2_gain: float32 [512], replicated, may hold values from 0.5 to 1.5
- norm2_shift: float32 [512], replicated, may hold values from -3 to 3
- tile_counts: int32 [36], replicated, may hold values from 1 to 64, 768 in all
- widths: int32 [36], replicated, may hold values from 32 to 128, as said below
Outputs:
- activated: float32 [196608, 512], P(('tiles', 'sub'))
Inputs may be any that keep to these rules, and one draw needn't show every extreme that they name: `widths`: each width is 128, 64 or 32; some image has width 128 and some has width 128 / 4. `tile_counts`: they add up to 768; the largest is 64.
All inputs are finite; a program needn't handle non-finite values.
Results may differ from a plain program's by a relative error of at most 0.00014.
Values sent between devices are 32-bit elements; how exact they have to be, the bound alone decides.
A program may use at most 128 MiB of HBM per device.

v0:
```python
import jax
import jax.numpy as jnp
from jax import lax
from jax.sharding import PartitionSpec as P

GROUPS = 32
WMAX = 128
TILE = 256


epsilon = 1e-06
highest = lax.Precision.HIGHEST


def extended(cells, sides, width):
    for axis, dim in sides:
        count = lax.axis_size(axis)
        ends = count - 1
        head = lax.slice_in_dim(cells, 0, width, axis=dim)
        tail = lax.slice_in_dim(cells, cells.shape[dim] - width, cells.shape[dim], axis=dim)
        cells = jnp.concatenate(
            [
                lax.ppermute(tail, axis, [(i, (i + 1) % count) for i in range(ends)]),
                cells,
                lax.ppermute(head, axis, [((i + 1) % count, i) for i in range(ends)]),
            ],
            axis=dim,
        )
    return cells


def pixel_layout(tile_counts, widths, pixels_here):
    device = lax.axis_index("tiles") * lax.axis_size("sub") + lax.axis_index("sub")
    pixel_counts = tile_counts * TILE
    image_ends = jnp.cumsum(pixel_counts)
    image_starts = image_ends - pixel_counts
    position = device * pixels_here + jnp.arange(pixels_here, dtype=jnp.int32)
    member = (position[None, :] >= image_starts[:, None]) & (
        position[None, :] < image_ends[:, None]
    )

    def per_pixel(per_image):
        return jnp.sum(jnp.where(member, per_image[:, None], 0), axis=0)

    pixel_width = per_pixel(widths)
    offset = position - per_pixel(image_starts)
    row_index = offset // pixel_width
    column_index = offset - row_index * pixel_width
    pixel_height = per_pixel(pixel_counts) // pixel_width
    return (
        member.astype(jnp.float32),
        pixel_counts,
        row_index,
        column_index,
        pixel_width,
        pixel_height,
    )


def group_table(per_channel):
    return jnp.sum(per_channel.reshape(per_channel.shape[0], GROUPS, -1), axis=2)


def spread_rows(onehot, per_image):
    return lax.dot_general(
        onehot,
        per_image,
        (((0,), (0,)), ((), ())),
        precision=highest,
        preferred_element_type=jnp.float32,
    )


def normalize(values, norm_gain, norm_shift, onehot, pixel_counts):
    group_size = values.shape[1] // GROUPS
    entries = (pixel_counts * group_size).astype(jnp.float32)[:, None]
    firsts = jnp.dot(onehot, values, precision=highest, preferred_element_type=jnp.float32)
    group_total = lax.psum(group_table(firsts), ("tiles", "sub"))
    group_mean = group_total / entries
    centred = values - spread_rows(onehot, jnp.repeat(group_mean, group_size, axis=1))
    seconds = jnp.dot(
        onehot, centred * centred, precision=highest, preferred_element_type=jnp.float32
    )
    spread = lax.psum(group_table(seconds), ("tiles", "sub")) / entries
    inverse = spread_rows(onehot, jnp.repeat(lax.rsqrt(spread + epsilon), group_size, axis=1))
    return jax.nn.silu(centred * inverse * norm_gain + norm_shift)


def shards(
    latents,
    conv_weight,
    conv_bias,
    norm1_gain,
    norm1_shift,
    norm2_gain,
    norm2_shift,
    tile_counts,
    widths,
):
    pixels_here = latents.shape[0]
    channels = latents.shape[1]
    onehot, pixel_counts, row_index, column_index, pixel_width, pixel_height = pixel_layout(
        tile_counts, widths, pixels_here
    )
    first_act = normalize(latents, norm1_gain, norm1_shift, onehot, pixel_counts)
    padded = extended(first_act.T, ((("tiles", "sub"), 1),), WMAX + 1)
    anchor = jnp.arange(pixels_here, dtype=jnp.int32) + (WMAX + 1)
    sources = []
    validity = []
    for step_y in (-1, 0, 1):
        for step_x in (-1, 0, 1):
            inside = (row_index + step_y >= 0) & (row_index + step_y < pixel_height)
            inside = inside & (column_index + step_x >= 0) & (column_index + step_x < pixel_width)
            sources.append(jnp.where(inside, anchor + step_y * pixel_width + step_x, anchor))
            validity.append(inside.astype(jnp.float32))
    all_sources = jnp.concatenate(sources)
    all_masks = jnp.concatenate(validity)
    tapped = jnp.take(padded, all_sources, axis=1) * all_masks[None, :]
    zero_sum = jnp.zeros((pixels_here, channels), jnp.float32)
    running = zero_sum
    weight_piece = lax.all_gather(conv_weight, "tiles", axis=0, tiled=True)
    row_count = weight_piece.shape[0]
    block_width = min(row_count, 128)
    for block_start in range(0, row_count, block_width):
        block_rows = min(block_width, row_count - block_start)
        taps_block = lax.dynamic_slice_in_dim(tapped, block_start, block_rows, 0)
        taps_block = taps_block.reshape(block_rows, 9, pixels_here)
        weight_block = weight_piece[block_start : block_start + block_rows]
        running = running + jnp.einsum(
            "ktp,kto->po",
            taps_block,
            weight_block,
            precision=highest,
            preferred_element_type=jnp.float32,
        )
    hidden = running
    hidden = hidden + conv_bias
    return normalize(hidden, norm2_gain, norm2_shift, onehot, pixel_counts)


def solution(mesh):
    return jax.shard_map(
        shards,
        mesh=mesh,
        in_specs=(
            P(("tiles", "sub"), None),
            P("tiles", None, None),
            P(),
            P(),
            P(),
            P(),
            P(),
            P(),
            P(),
        ),
        out_specs=P(("tiles", "sub"), None),
        check_vma=False,
    )
```

profile of v0, /device:TPU:1, one launch (start us, length us, event | category | flops | bytes accessed | tf_op | source)
XLA Modules:
  0.0 433.0 jit_solution(8447993397408596706)
XLA Ops:
  6.5 0.0 copy-start.3
  6.5 0.0 all-gather.2.cloned.1.call-start
  6.5 0.7 all-gather.2.cloned.1.call-update
  7.3 0.7 broadcast_multiply_fusion
  7.9 0.1 copy.16
  8.0 0.1 reduce-window.8
  8.1 0.1 reduce
  8.2 0.7 fusion.25
  8.9 2.8 bitcast_reduce_fusion.3
  11.7 83.9 %psum.28 = f32[36,32]{0,1:T(8,128)S(1)} all-reduce(f32[36,32]{0,1:T(8,128)S(1)} %bitcast_reduce_fusion.3), channel_id=1, replica_groups=mesh['tiles'=32,'sub'=8] {'tiles','sub'}, use_global_device_ids=true, to_apply=%region_5.6 | all-reduce | flops 1152 | bytes 9216 | tf_op jit(solution)/shard_map/psum | solution.py:78
  95.6 0.0 copy-done.3
  95.7 0.9 convolution_subtract_fusion.1
  96.6 0.0 copy-start.7
  96.6 0.0 copy-start.8
  96.6 1.4 bitcast_reduce_fusion.2
  98.0 73.4 %psum.29 = f32[36,32]{0,1:T(8,128)S(1)} all-reduce(f32[36,32]{0,1:T(8,128)S(1)} %bitcast_reduce_fusion.2), channel_id=1, replica_groups=mesh['tiles'=32,'sub'=8] {'tiles','sub'}, use_global_device_ids=true, to_apply=%region_7.8 | all-reduce | flops 1152 | bytes 9216 | tf_op jit(solution)/shard_map/psum | solution.py:84
  171.5 0.0 copy-done.7
  171.5 0.0 copy-done.8
  171.5 0.0 copy-start.6
  171.5 1.3 multiply_bitcast_fusion.1
  172.8 0.0 copy-start.4
  172.8 1.1 copy-done.4
  174.0 3.2 collective-permute-start
  177.2 13.6 %collective-permute-start.1 = (f32[512,129]{0,1:T(8,128)S(1)}, f32[512,129]{0,1:T(8,128)S(1)}, u32[]{:S(2)}, u32[]{:S(2)}) collective-permute-start(f32[512,129]{0,1:T(8,128)S(1)} %get-tuple-element.43), channel_id=1, source_target_pairs={{1,0},{2,1},{3,2},{4,3},{5,4},{6,5},{7,6},{8,7},{9,8},{10,9},{11,1... | collective-permute-start | bytes 792584 | tf_op jit(solution)/shard_map/ppermute | solution.py:25
  190.8 0.0 copy-done.6
  190.8 0.1 select_reduce_fusion
  190.9 0.1 constant_dynamic-update-slice_fusion
  191.1 0.2 dynamic-update-slice
  191.3 0.2 dynamic-update-slice.1
  191.6 0.2 dynamic-update-slice.2
  191.8 0.1 constant_dynamic-update-slice_fusion.16
  191.9 0.2 dynamic-update-slice.3
  192.2 0.2 dynamic-update-slice.4
  192.4 0.2 dynamic-update-slice.5
  192.7 0.1 constant_dynamic-update-slice_fusion.13
  192.8 0.2 dynamic-update-slice.6
  193.1 0.2 dynamic-update-slice.7
  193.5 0.1 fusion.19
  193.6 0.0 collective-permute-done
  193.6 0.0 collective-permute-done.1
  193.6 4.5 %concatenate.54 = f32[512,1026]{0,1:T(8,128)S(1)} concatenate(f32[512,129]{0,1:T(8,128)S(1)} %collective-permute-done, f32[512,768]{0,1:T(8,128)} %copy-done.4, f32[512,129]{0,1:T(8,128)S(1)} %collective-permute-done.1), dimensions={1} | concatenate | bytes 4202496 | tf_op jit(solution)/shard_map/concatenate | solution.py:21
  198.1 18.6 %gather_fusion = f32[6912,512]{1,0:T(8,128)} fusion(f32[512,1026]{0,1:T(8,128)S(1)} %concatenate.54, s32[7168]{0:T(1024)S(1)} %pad_clamp_fusion), kind=kCustom, calls=%fused_computation | custom fusion | bytes 28339200 | tf_op jit(solution)/shard_map/jit(_take)/gather | solution.py:118
  216.7 11.6 %multiply_bitcast_fusion = f32[512,6912]{0,1:T(8,128)} fusion(f32[6912,512]{1,0:T(8,128)} %gather_fusion, f32[6912]{0:T(1024)S(1)} %concatenate.66, pred[6912]{0:T(1024)(128)(4,1)S(1)} %compare_and_fusion.1), kind=kLoop, calls=%fused_computation.1 | loop fusion | flops 7077888 | bytes 28346112 | tf_op jit(solution)/shard_map/mul | solution.py:118
  228.3 9.4 %fusion.35 = (f32[128,6912]{0,1:T(8,128)}, f32[128,6912]{0,1:T(8,128)}, f32[128,6912]{0,1:T(8,128)}, f32[128,6912]{0,1:T(8,128)S(1)}) fusion(f32[512,6912]{0,1:T(8,128)} %multiply_bitcast_fusion), kind=kLoop, calls=%fused_computation.106 | loop fusion | bytes 28311552 | tf_op jit(solution)/shard_map/dynamic_slice | solution.py:126
  237.7 9.2 %fusion = f32[768,512,1]{1,0,2:T(8,128)S(1)} fusion(f32[128,9,768]{0,2,1:T(8,128)} %bitcast.48, f32[512,9,512]{2,0,1:T(8,128)} %all-gather.2.cloned.1.call-done), kind=kOutput, calls=%fused_computation.2 | convolution fusion | flops 5435817984 | bytes 7471104 | tf_op jit(solution)/shard_map/ktp,kto->po/dot_general | solution.py:129
  246.8 0.0 copy-done
  246.9 8.0 %fusion.2 = f32[768,512,1]{1,0,2:T(8,128)S(1)} fusion(f32[128,9,768]{0,2,1:T(8,128)S(1)} %bitcast.47, f32[512,9,512]{2,0,1:T(8,128)} %all-gather.2.cloned.1.call-done), kind=kOutput, calls=%fused_computation.4 | convolution fusion | flops 5435817984 | bytes 7471104 | tf_op jit(solution)/shard_map/ktp,kto->po/dot_general | solution.py:129
  254.8 0.0 copy-done.2
  254.8 0.0 copy-start.1
  254.9 0.0 copy-start.5
  254.9 6.5 %fusion.4 = f32[768,512,1]{1,0,2:T(8,128)S(1)} fusion(f32[128,9,768]{0,2,1:T(8,128)S(1)} %bitcast.46, f32[512,9,512]{2,0,1:T(8,128)S(1)} %copy-done.2), kind=kOutput, calls=%fused_computation.6 | convolution fusion | flops 5435817984 | bytes 7471104 | tf_op jit(solution)/shard_map/ktp,kto->po/dot_general | solution.py:129
  261.4 0.0 copy-done.1
  261.4 0.0 copy-done.5
  261.4 6.4 %fusion.8 = f32[768,512]{1,0:T(8,128)S(1)} fusion(f32[768,512,1]{1,0,2:T(8,128)S(1)} %fusion, f32[768,512,1]{1,0,2:T(8,128)S(1)} %fusion.2, f32[768,512,1]{1,0,2:T(8,128)S(1)} %fusion.4, f32[128,9,768]{0,2,1:T(8,128)S(1)} %bitcast.49, f32[512,9,512]{2,0,1:T(8,128)S(1)} %copy-done.2, f32[512]{0:T(512)S(1)} %copy-done.5), kind=kOutput, calls=%fused_computation.11 | convolution fusion | flops 5437390848 | bytes 12191744 | tf_op jit(solution)/shard_map/ktp,kto->po/dot_general | solution.py:129
  267.8 1.4 bitcast_reduce_fusion.1
  269.2 77.3 %psum.30 = f32[36,32]{0,1:T(8,128)S(1)} all-reduce(f32[36,32]{0,1:T(8,128)S(1)} %bitcast_reduce_fusion.1), channel_id=1, replica_groups=mesh['tiles'=32,'sub'=8] {'tiles','sub'}, use_global_device_ids=true, to_apply=%region_9.10 | all-reduce | flops 1152 | bytes 9216 | tf_op jit(solution)/shard_map/psum | solution.py:78
  346.5 0.9 convolution_subtract_fusion
  347.5 0.0 copy-start.9
  347.5 0.0 copy-start.10
  347.5 1.4 bitcast_reduce_fusion
  348.9 74.3 %psum.31 = f32[36,32]{0,1:T(8,128)S(1)} all-reduce(f32[36,32]{0,1:T(8,128)S(1)} %bitcast_reduce_fusion), channel_id=1, replica_groups=mesh['tiles'=32,'sub'=8] {'tiles','sub'}, use_global_device_ids=true, to_apply=%region_11.12 | all-reduce | flops 1152 | bytes 9216 | tf_op jit(solution)/shard_map/psum | solution.py:84
  423.3 0.0 copy-done.9
  423.3 0.0 copy-done.10
  423.3 2.4 divide_multiply_fusion
  (37 shorter events, 0.4 us)
Async XLA Ops:
  6.5 89.1 %copy-start.3 = (f32[768,512]{1,0:T(8,128)S(1)}, f32[768,512]{1,0:T(8,128)}, u32[]{:S(2)}) copy-start(f32[768,512]{1,0:T(8,128)} %param.9) | copy-start | bytes 4718596
  6.5 231.1 %all-gather.2.cloned.1.call-start = ((), (), s32[]{:S(2)}) async-start(), calls=%async_computation | async-start | bytes 9732096 | tf_op jit(solution)/shard_map/all_gather | solution.py:121
  96.6 74.9 %copy-start.7 = (f32[512]{0:T(512)S(1)}, f32[512]{0:T(512)}, u32[]{:S(2)}) copy-start(f32[512]{0:T(512)} %param.13) | copy-start | bytes 6148
  96.6 74.9 %copy-start.8 = (f32[512]{0:T(512)S(1)}, f32[512]{0:T(512)}, u32[]{:S(2)}) copy-start(f32[512]{0:T(512)} %param.12) | copy-start | bytes 6148
  171.5 19.3 %copy-start.6 = (s32[36]{0:T(128)S(1)}, s32[36]{0:T(128)}, u32[]{:S(2)}) copy-start(s32[36]{0:T(128)} %param.17) | copy-start | bytes 436
  172.8 1.1 copy-start.4
  174.0 19.7 %collective-permute-start = (f32[512,129]{0,1:T(8,128)S(1)}, f32[512,129]{0,1:T(8,128)S(1)}, u32[]{:S(2)}, u32[]{:S(2)}) collective-permute-start(f32[512,129]{0,1:T(8,128)S(1)} %get-tuple-element.44), channel_id=1, source_target_pairs={{0,1},{1,2},{2,3},{3,4},{4,5},{5,6},{6,7},{7,8},{8,9},{9,10},{10,1... | collective-permute-start | bytes 792584 | tf_op jit(solution)/shard_map/ppermute | solution.py:23
  177.2 16.4 %collective-permute-start.1 = (f32[512,129]{0,1:T(8,128)S(1)}, f32[512,129]{0,1:T(8,128)S(1)}, u32[]{:S(2)}, u32[]{:S(2)}) collective-permute-start(f32[512,129]{0,1:T(8,128)S(1)} %get-tuple-element.43), channel_id=1, source_target_pairs={{1,0},{2,1},{3,2},{4,3},{5,4},{6,5},{7,6},{8,7},{9,8},{10,9},{11,1... | collective-permute-start | bytes 792584 | tf_op jit(solution)/shard_map/ppermute | solution.py:25
  237.7 9.2 %copy-start = (f32[128,6912]{0,1:T(8,128)S(1)}, f32[128,6912]{0,1:T(8,128)}, u32[]{:S(2)}) copy-start(f32[128,6912]{0,1:T(8,128)} %get-tuple-element.41) | copy-start | bytes 10616836
  237.7 17.2 %copy-start.2 = (f32[512,9,512]{2,0,1:T(8,128)S(1)}, f32[512,9,512]{2,0,1:T(8,128)}, u32[]{:S(2)}) copy-start(f32[512,9,512]{2,0,1:T(8,128)} %all-gather.2.cloned.1.call-done) | copy-start | bytes 28311556
  254.8 6.5 %copy-start.1 = (f32[128,6912]{0,1:T(8,128)S(1)}, f32[128,6912]{0,1:T(8,128)}, u32[]{:S(2)}) copy-start(f32[128,6912]{0,1:T(8,128)} %get-tuple-element.39) | copy-start | bytes 10616836
  254.9 6.5 %copy-start.5 = (f32[512]{0:T(512)S(1)}, f32[512]{0:T(512)}, u32[]{:S(2)}) copy-start(f32[512]{0:T(512)} %param.11) | copy-start | bytes 6148
  347.5 75.8 %copy-start.9 = (f32[512]{0:T(512)S(1)}, f32[512]{0:T(512)}, u32[]{:S(2)}) copy-start(f32[512]{0:T(512)} %param.15) | copy-start | bytes 6148
  347.5 75.8 %copy-start.10 = (f32[512]{0:T(512)S(1)}, f32[512]{0:T(512)}, u32[]{:S(2)}) copy-start(f32[512]{0:T(512)} %param.14) | copy-start | bytes 6148
Sparse Core Ops, SparseCore 0:
  9.9 107.1 all-gather.1
where the time goes:
time: 436 us; the launch traced here: 433 us
  blocking collectives  309 us (71%)
  matrix products  42.7 us (10%)
  local copies, waits for them, and re-layouts  35.8 us (8%)
  starting transfers between devices  16.8 us (4%)
  between operations  14.3 us (3%)
  other arithmetic  13.9 us (3%)
    psum x2, blocking collectives, normalize(): group_total = lax.psum(group_table(firsts), ('tiles', 'sub'))  161 us
    psum x2, blocking collectives, normalize(): spread = lax.psum(group_table(seconds), ('tiles', 'sub')) / entries  148 us
    dot_general x4, matrix products, shards(): jnp.einsum('ktp,kto->po', taps_block, weight_block, precision=highest, pr...  30 us
    gather x1, local copies, waits for them, and re-layouts, shards(): tapped = jnp.take(padded, all_sources, axis=1) * all_masks[None, :]  18.6 us
    ppermute x1, starting transfers between devices, extended(): lax.ppermute(head, axis, [((i + 1) % count, i) for i in range(ends)])  13.6 us
    mul x1, other arithmetic, shards(): tapped = jnp.take(padded, all_sources, axis=1) * all_masks[None, :]  11.6 us
    dynamic_slice x1, local copies, waits for them, and re-layouts, shards(): taps_block = lax.dynamic_slice_in_dim(tapped, block_start, block_rows, 0)  9.35 us
  transfers between devices with their start and end apart: 3, of which 0 were waited for; matrix products, arithmetic and copies ran while one was open for 13% of the time, Pallas kernels for 0%

commit v1 on v0

v1 whole, which is shorter than its diff:
```python
import functools

import jax
import jax.numpy as jnp
from jax import lax
from jax.experimental import pallas as pl
from jax.experimental.pallas import tpu as pltpu
from jax.sharding import PartitionSpec as P

MESH = pl.DeviceIdType.MESH
F32 = jnp.float32
BF16 = jnp.bfloat16

TILE = 256
GROUP = 16
HALF = 128
EPS = 1e-06
WINDOW = 21
PEERS = 2 * WINDOW
A_TAPS = (0, 4)
B_TAPS = (4, 5)
FULL, LOW, HIGH = 0, 1, 2


def lane_iota(shape):
    return lax.broadcasted_iota(jnp.int32, shape, len(shape) - 1)


def butterfly(values, step):
    lanes = lane_iota(values.shape)
    up = pltpu.roll(values, step, 1)
    down = pltpu.roll(values, HALF - step, 1)
    return values + jnp.where((lanes & step) != 0, up, down)


def fold_lanes(rows):
    return jnp.concatenate([rows[:, HALF * b : HALF * (b + 1)] for b in range(4)], axis=0)


def unfold_lanes(folded):
    return jnp.concatenate([folded[8 * b : 8 * (b + 1)] for b in range(4)], axis=1)


def group_sum(rows):
    folded = fold_lanes(rows)
    for step in (1, 2, 4, 8):
        folded = butterfly(folded, step)
    return folded


def pack_groups(folded):
    lanes = lane_iota((8, HALF))
    packed = jnp.zeros((8, HALF), F32)
    for b in range(4):
        packed = jnp.where((lanes & 3) == b, folded[8 * b : 8 * (b + 1)], packed)
    return packed


def unpack_groups(packed):
    lanes = lane_iota((8, HALF))
    blocks = []
    for b in range(4):
        block = jnp.where((lanes & 3) == b, packed, 0.0)
        block = butterfly(butterfly(block, 1), 2)
        blocks.append(block)
    return jnp.concatenate(blocks, axis=1)


def rows_of(parts):
    zeros = jnp.zeros((8 - len(parts), parts[0].shape[1]), F32)
    return jnp.concatenate(parts + [zeros], axis=0)


def tile_stats(ref):
    sums = rows_of(
        [jnp.sum(ref[TILE * j : TILE * (j + 1), :], axis=0, keepdims=True) for j in range(3)]
    )
    total = group_sum(sums)
    means = unfold_lanes(total * (1.0 / (TILE * GROUP)))
    seconds = []
    for j in range(3):
        off = ref[TILE * j : TILE * (j + 1), :] - means[j : j + 1]
        seconds.append(jnp.sum(off * off, axis=0, keepdims=True))
    spread = group_sum(rows_of(seconds))
    return pack_groups(total) + pltpu.roll(pack_groups(spread), 4, 0)


def image_stats(win, stat, me, starts, ends):
    rows = win.shape[0] + 8
    table = jnp.concatenate([win[...], stat[...]], axis=0)
    row = lax.broadcasted_iota(jnp.int32, (rows, HALF), 0)
    slot = row >> 3
    tile_row = row & 7
    offset = jnp.where(slot >= WINDOW, slot - WINDOW + 1, slot - WINDOW)
    offset = jnp.where(slot >= PEERS, 0, offset)
    tile = 3 * (me + offset) + tile_row
    second = pltpu.roll(table.reshape(rows // 8, 8, HALF), 4, 1).reshape(rows, HALF)
    tile_mean = table * (1.0 / (TILE * GROUP))
    means, inverses = [], []
    for j in range(3):
        member = (tile >= starts[j]) & (tile < ends[j]) & (tile_row < 3)
        count = jnp.full((1, HALF), (ends[j] - starts[j]) * (TILE * GROUP), jnp.int32).astype(F32)
        mean = jnp.sum(jnp.where(member, table, 0.0), axis=0, keepdims=True) / count
        away = tile_mean - mean
        moment = second + (TILE * GROUP) * (away * away)
        spread = jnp.sum(jnp.where(member, moment, 0.0), axis=0, keepdims=True) / count
        means.append(mean)
        inverses.append(lax.rsqrt(spread + EPS))
    packed = rows_of(means) + pltpu.roll(rows_of(inverses), 4, 0)
    return unpack_groups(packed)


def kernel(
    counts,
    widths,
    latents,
    weight,
    bias,
    gain,
    shift,
    hidden,
    coef_out,
    local,
    halo,
    taps_a,
    taps_b,
    acts,
    total,
    w_high,
    w_low,
    coef,
    stat1,
    stat2,
    win1,
    win2,
    local_sem,
    halo_send,
    halo_recv,
    stat_send,
    stat_recv,
    send_sem,
    ax_recv,
    az_recv,
    bz_recv,
    bx_recv,
    pair_recv,
):
    t = lax.axis_index("tiles")
    s = lax.axis_index("sub")
    me = t * 8 + s
    z, x = t // 4, t % 4
    core = s % 2

    def at(index):
        p = lax.rem(index + 256, 256)
        return (p // 8, p % 8)

    right = {
        "z+": (lax.rem(z + 1, 8) * 4 + x, s),
        "z-": (lax.rem(z + 7, 8) * 4 + x, s),
        "x+": (z * 4 + lax.rem(x + 1, 4), s),
        "x-": (z * 4 + lax.rem(x + 3, 4), s),
        "c": (t, s + 1 - 2 * core),
    }

    def z_row(dz):
        return lax.rem(z + dz + 8, 8) * 4

    def row_of(dz, dx):
        return z_row(dz) + lax.rem(x + dx + 4, 4)

    barrier = pltpu.get_barrier_semaphore()

    def greet(step, carry):
        for sign in (1, -1):
            pl.semaphore_signal(barrier, inc=1, device_id=at(me + sign * step), device_id_type=MESH)
        return carry

    for name in ("z+", "z-", "x+", "x-"):
        pl.semaphore_signal(barrier, inc=1, device_id=right[name], device_id_type=MESH)
    lax.fori_loop(1, WINDOW + 1, greet, 0)

    load = pltpu.make_async_copy(latents, local, local_sem.at[0])
    load.start()

    own = [
        pltpu.make_async_copy(weight.at[pl.ds(0, 4)], taps_a.at[t], local_sem.at[1]),
        pltpu.make_async_copy(weight.at[pl.ds(4, 5)], taps_b.at[t], local_sem.at[1]),
    ]
    for owner in range(2):
        pl.when(core == owner)(own[owner].start)

    tiles = [3 * me + j for j in range(3)]
    starts = [me * 0] * 3
    ends = [me * 0] * 3
    width = [me * 0 + 32] * 3
    begin = me * 0

    def place(i, carry):
        begin, starts, ends, width = carry
        end = begin + counts[i]
        inside = [(tile >= begin) & (tile < end) for tile in tiles]
        starts = [jnp.where(hit, begin, old) for hit, old in zip(inside, starts)]
        ends = [jnp.where(hit, end, old) for hit, old in zip(inside, ends)]
        width = [jnp.where(hit, widths[i], old) for hit, old in zip(inside, width)]
        return end, starts, ends, width

    _, starts, ends, width = lax.fori_loop(
        0, counts.shape[0], place, (begin, starts, ends, width)
    )

    def piece(taps, first, count):
        if taps[0] < 4:
            return taps_a.at[pl.ds(first, count), pl.ds(taps[0], taps[1])]
        return taps_b.at[pl.ds(first, count), pl.ds(taps[0] - 4, taps[1])]

    sent = {0: [], 1: []}

    def send(owner, taps, first, count, way, recv):
        ref = piece(taps, first, count)
        copy = pltpu.make_async_remote_copy(
            src_ref=ref,
            dst_ref=ref,
            send_sem=send_sem.at[len(sent[owner])],
            recv_sem=recv,
            device_id=right[way],
            device_id_type=MESH,
        )
        copy.start()
        sent[owner].append((taps, count))

    def arrived(taps, first, count, recv):
        ref = piece(taps, first, count)
        pltpu.make_async_remote_copy(
            src_ref=ref,
            dst_ref=ref,
            send_sem=send_sem.at[0],
            recv_sem=recv,
            device_id=right["c"],
            device_id_type=MESH,
        ).wait_recv()

    group_of = {0: 0, -1: 1, 1: 2, -2: 3, 2: 4, -3: 5, 3: 6, 4: 7}
    a_low, a_high = (0, 2), (2, 2)
    b_low, b_high = (4, 2), (6, 3)

    def a_start():
        own[0].wait()
        send(0, A_TAPS, row_of(0, 0), 1, "x+", ax_recv.at[0])
        send(0, A_TAPS, row_of(0, 0), 1, "x-", ax_recv.at[1])

    def a_x_near():
        arrived(A_TAPS, row_of(0, -1), 1, ax_recv.at[0])
        send(0, a_low, row_of(0, -1), 1, "x+", ax_recv.at[2])
        arrived(A_TAPS, row_of(0, 1), 1, ax_recv.at[1])
        send(0, a_high, row_of(0, 1), 1, "x-", ax_recv.at[3])

    def a_x_far():
        arrived(a_low, row_of(0, 2), 1, ax_recv.at[2])
        arrived(a_high, row_of(0, 2), 1, ax_recv.at[3])
        for h in range(2):
            send(0, A_TAPS, z_row(0) + 2 * h, 2, "z+", az_recv.at[h])
            send(0, A_TAPS, z_row(0) + 2 * h, 2, "z-", az_recv.at[6 + h])
        send(0, A_TAPS, z_row(0), 4, "c", pair_recv.at[0])

    def a_z(d):
        if d == 4:
            arrived(A_TAPS, z_row(4), 2, az_recv.at[12])
            arrived(A_TAPS, z_row(4) + 2, 2, az_recv.at[13])
            send(0, A_TAPS, z_row(4), 4, "c", pair_recv.at[7])
            return
        for h in range(2):
            for way in range(2):
                dz = d if way else -d
                row = z_row(dz) + 2 * h
                arrived(A_TAPS, row, 2, az_recv.at[way * 6 + (d - 1) * 2 + h])
                if d < 3:
                    send(0, A_TAPS, row, 2, "z-" if way else "z+", az_recv.at[way * 6 + d * 2 + h])
                elif way == h:
                    send(0, A_TAPS, row, 2, "z-" if way else "z+", az_recv.at[12 + h])
        for dz in (-d, d):
            send(0, A_TAPS, z_row(dz), 4, "c", pair_recv.at[group_of[dz]])

    def b_spread(dz):
        g = group_of[dz]
        send(1, B_TAPS, row_of(dz, 0), 1, "x+", bx_recv.at[4 * g])
        send(1, B_TAPS, row_of(dz, 0), 1, "x-", bx_recv.at[4 * g + 1])

    def b_start():
        own[1].wait()
        send(1, B_TAPS, row_of(0, 0), 1, "z+", bz_recv.at[0])
        send(1, B_TAPS, row_of(0, 0), 1, "z-", bz_recv.at[3])
        b_spread(0)

    def b_z(d):
        if d == 4:
            arrived(b_low, row_of(4, 0), 1, bz_recv.at[6])
            arrived(b_high, row_of(4, 0), 1, bz_recv.at[7])
            b_spread(4)
            return
        for way in range(2):
            dz = d if way else -d
            arrived(B_TAPS, row_of(dz, 0), 1, bz_recv.at[way * 3 + d - 1])
            if d < 3:
                send(1, B_TAPS, row_of(dz, 0), 1, "z-" if way else "z+", bz_recv.at[way * 3 + d])
            else:
                taps = b_high if way else b_low
                send(1, taps, row_of(dz, 0), 1, "z-" if way else "z+", bz_recv.at[6 + way])
            b_spread(dz)

    def b_near(dz):
        g = group_of[dz]
        arrived(B_TAPS, row_of(dz, -1), 1, bx_recv.at[4 * g])
        send(1, b_low, row_of(dz, -1), 1, "x+", bx_recv.at[4 * g + 2])
        arrived(B_TAPS, row_of(dz, 1), 1, bx_recv.at[4 * g + 1])
        send(1, b_high, row_of(dz, 1), 1, "x-", bx_recv.at[4 * g + 3])

    def b_far(dz):
        g = group_of[dz]
        arrived(b_low, row_of(dz, 2), 1, bx_recv.at[4 * g + 2])
        arrived(b_high, row_of(dz, 2), 1, bx_recv.at[4 * g + 3])
        send(1, B_TAPS, z_row(dz), 4, "c", pair_recv.at[g])

    def serve(a_steps, b_steps):
        @pl.when(core == 0)
        def _():
            for step in a_steps:
                step()

        @pl.when(core == 1)
        def _():
            for step in b_steps:
                step()

    def pair_arrived(groups):
        @pl.when(core == 0)
        def _():
            for dz in groups:
                arrived(B_TAPS, z_row(dz), 4, pair_recv.at[group_of[dz]])

        @pl.when(core == 1)
        def _():
            for dz in groups:
                arrived(A_TAPS, z_row(dz), 4, pair_recv.at[group_of[dz]])

    do = functools.partial

    load.wait()
    stat1[...] = tile_stats(local)
    for h in range(8):
        rows = pl.ds(96 * h, 96)
        total[rows, :] = jnp.broadcast_to(bias[...], (96, 512))

    pl.semaphore_wait(barrier, PEERS + 4)
    serve([a_start], [b_start])
    up = pltpu.make_async_remote_copy(
        src_ref=latents.at[pl.ds(5 * HALF, HALF), :],
        dst_ref=halo.at[0],
        send_sem=halo_send.at[0],
        recv_sem=halo_recv.at[0],
        device_id=at(me + 1),
        device_id_type=MESH,
    )
    down = pltpu.make_async_remote_copy(
        src_ref=latents.at[pl.ds(0, HALF), :],
        dst_ref=halo.at[1],
        send_sem=halo_send.at[1],
        recv_sem=halo_recv.at[1],
        device_id=at(me - 1),
        device_id_type=MESH,
    )

    def share(stat, win, which):
        def one(step, carry):
            for slot, to in ((WINDOW - step, me + step), (WINDOW - 1 + step, me - step)):
                pltpu.make_async_remote_copy(
                    src_ref=stat,
                    dst_ref=win.at[pl.ds(pl.multiple_of(slot * 8, 8), 8), :],
                    send_sem=stat_send.at[which],
                    recv_sem=stat_recv.at[which],
                    device_id=at(to),
                    device_id_type=MESH,
                ).start()
            return carry

        lax.fori_loop(1, WINDOW + 1, one, 0)

    def collect(win, which):
        ref = win
        both = pltpu.make_async_remote_copy(
            src_ref=ref,
            dst_ref=ref,
            send_sem=stat_send.at[which],
            recv_sem=stat_recv.at[which],
            device_id=at(me + 1),
            device_id_type=MESH,
        )
        both.wait_send()
        both.wait_recv()

    share(stat1, win1, 0)
    up.start()
    down.start()
    serve([a_x_near], [do(b_z, 1), do(b_near, 0)])
    serve([a_x_far], [do(b_z, 2), do(b_far, 0), do(b_near, -1), do(b_near, 1)])
    collect(win1, 0)
    coef[...] = image_stats(win1, stat1, me, starts, ends)
    up.wait()
    down.wait()

    def act_block(source, j, wide, stores):
        row = lax.broadcasted_iota(jnp.int32, (HALF, HALF), 0)
        column = row & (wide - 1)
        has_left = column != 0
        has_right = column != wide - 1
        for b in range(4):
            lanes = pl.ds(HALF * b, HALF)
            mean = coef[pl.ds(j, 1), lanes]
            scale = coef[pl.ds(j + 4, 1), lanes] * gain[:, HALF * b : HALF * (b + 1)]
            value = (source(lanes) - mean) * scale + shift[:, HALF * b : HALF * (b + 1)]
            act = value / (1.0 + jnp.exp(-value))
            shifted = (
                jnp.where(has_left, pltpu.roll(act, 1, 0), 0.0),
                act,
                jnp.where(has_right, pltpu.roll(act, HALF - 1, 0), 0.0),
            )
            for dx in range(3):
                high = shifted[dx].astype(BF16)
                low = (shifted[dx] - high.astype(F32)).astype(BF16)
                for base, valid in stores:
                    rows = pl.ds(base, HALF)
                    if valid is None:
                        acts[dx, 0, rows, lanes] = high
                        acts[dx, 1, rows, lanes] = low
                    else:
                        keep = jnp.where(valid, 1.0, 0.0).astype(F32)
                        acts[dx, 0, rows, lanes] = (high.astype(F32) * keep).astype(BF16)
                        acts[dx, 1, rows, lanes] = (low.astype(F32) * keep).astype(BF16)

    act_block(lambda lanes: halo[0, :, lanes], 0, width[0], [(0, tiles[0] > starts[0])])
    act_block(lambda lanes: halo[1, :, lanes], 2, width[2], [(2 * 512 + 384, tiles[2] + 1 < ends[2])])
    for q in range(6):
        j, half = q // 2, q % 2
        stores = [(j * 512 + HALF + half * HALF, None)]
        if half == 0 and j > 0:
            stores.append(((j - 1) * 512 + 384, tiles[j] > starts[j]))
        if half == 1 and j < 2:
            stores.append(((j + 1) * 512, tiles[j + 1] > starts[j + 1]))
        act_block(lambda lanes, q=q: local[HALF * q : HALF * (q + 1), lanes], j, width[j], stores)

    serve(
        [do(a_z, 1)],
        [do(b_z, 3), do(b_far, -1), do(b_far, 1), do(b_near, -2), do(b_near, 2)],
    )

    odd = z % 2
    first = z // 2
    order = [
        first,
        lax.rem(first + 3 + 2 * odd, 4),
        lax.rem(first + 1 + 2 * odd, 4),
        lax.rem(first + 2, 4),
    ]
    groups = [(0, -1, 1), (-2, 2), (-3, 3), (4,)]

    def split_weights(chunk):
        def fixed(c):
            for source, skip in ((taps_a, 0), (taps_b, 4)):
                for tap in range(source.shape[1]):
                    value = source[8 * c : 8 * c + 8, tap : tap + 1].reshape(HALF, 512)
                    to = pl.ds((tap + skip) * HALF, HALF)
                    high = value.astype(BF16)
                    w_high[to, :] = high
                    w_low[to, :] = (value - high.astype(F32)).astype(BF16)

        for c in range(4):
            pl.when(chunk == c)(functools.partial(fixed, c))

    def multiply(chunk, j):
        lanes = pl.ds(pl.multiple_of(chunk * HALF, HALF), HALF)
        wide = width[j]

        is_wide, is_middle = wide == 128, wide == 64

        def taps(part):
            columns = []
            for dy in (-1, 0, 1):
                for dx in range(3):
                    base = j * 512 + HALF
                    if dy == 0:
                        columns.append(acts[dx, part, pl.ds(base, TILE), lanes])
                        continue
                    near = acts[dx, part, pl.ds(base + 32 * dy, TILE), lanes]
                    middle = acts[dx, part, pl.ds(base + 64 * dy, TILE), lanes]
                    far = acts[dx, part, pl.ds(base + 128 * dy, TILE), lanes]
                    columns.append(
                        jnp.where(is_wide, far, jnp.where(is_middle, middle, near))
                    )
            return jnp.concatenate(columns, axis=1)

        high = taps(0)
        low = taps(1)
        out = jnp.dot(high, w_high[...], preferred_element_type=F32)
        out += jnp.dot(low, w_high[...], preferred_element_type=F32)
        out += jnp.dot(high, w_low[...], preferred_element_type=F32)
        rows = pl.ds(pl.multiple_of(j * TILE, TILE), TILE)
        total[rows, :] += out

    between = {
        (0, 0): ([], [do(b_z, 4)]),
        (0, 1): ([], [do(b_far, -2), do(b_far, 2)]),
        (0, 2): ([do(a_z, 2)], [do(b_near, -3), do(b_near, 3)]),
        (1, 0): ([], [do(b_far, -3), do(b_far, 3)]),
        (1, 1): ([], [do(b_near, 4)]),
        (1, 2): ([do(a_z, 3)], [do(b_far, 4)]),
        (2, 2): ([do(a_z, 4)], []),
    }

    for k in range(4):
        pair_arrived(groups[k])
        split_weights(order[k])
        for j in range(3):
            multiply(order[k], j)
            if (k, j) in between:
                serve(*between[(k, j)])

    store = pltpu.make_async_copy(total, hidden, local_sem.at[6])
    store.start()
    stat2[...] = tile_stats(total)
    share(stat2, win2, 1)
    for owner in range(2):

        @pl.when(core == owner)
        def _(owner=owner):
            for index, (taps, count) in enumerate(sent[owner]):
                ref = piece(taps, z_row(0), count)
                pltpu.make_async_remote_copy(
                    src_ref=ref,
                    dst_ref=ref,
                    send_sem=send_sem.at[index],
                    recv_sem=pair_recv.at[0],
                    device_id=right["c"],
                    device_id_type=MESH,
                ).wait_send()

    collect(win2, 1)
    coef_out[...] = image_stats(win2, stat2, me, starts, ends)
    store.wait()


def shards(latents, weight, bias, gain1, shift1, gain2, shift2, tile_counts, widths):
    vmem = pl.BlockSpec(memory_space=pltpu.VMEM)
    smem = pl.BlockSpec(memory_space=pltpu.SMEM)
    hbm = pl.BlockSpec(memory_space=pl.ANY)
    dma = pltpu.SemaphoreType.DMA
    pixels, channels = latents.shape
    hidden, coef = pl.pallas_call(
        kernel,
        out_shape=(
            jax.ShapeDtypeStruct((pixels, channels), F32),
            jax.ShapeDtypeStruct((8, channels), F32),
        ),
        in_specs=[smem, smem, hbm, hbm, vmem, vmem, vmem],
        out_specs=(hbm, vmem),
        scratch_shapes=[
            pltpu.VMEM((pixels, channels), F32),
            pltpu.VMEM((2, HALF, channels), F32),
            pltpu.VMEM((32, 4, 16, channels), F32),
            pltpu.VMEM((32, 5, 16, channels), F32),
            pltpu.VMEM((3, 2, 1536, channels), BF16),
            pltpu.VMEM((pixels, channels), F32),
            pltpu.VMEM((9 * HALF, channels), BF16),
            pltpu.VMEM((9 * HALF, channels), BF16),
            pltpu.VMEM((8, channels), F32),
            pltpu.VMEM((8, HALF), F32),
            pltpu.VMEM((8, HALF), F32),
            pltpu.VMEM((8 * PEERS, HALF), F32),
            pltpu.VMEM((8 * PEERS, HALF), F32),
            dma((7,)),
            dma((2,)),
            dma((2,)),
            dma((2,)),
            dma((2,)),
            dma((48,)),
            dma((4,)),
            dma((14,)),
            dma((8,)),
            dma((32,)),
            dma((8,)),
        ],
        compiler_params=pltpu.CompilerParams(
            collective_id=0, has_side_effects=True, vmem_limit_bytes=60 << 20
        ),
        name="block",
    )(
        tile_counts,
        widths,
        latents,
        jnp.transpose(weight, (1, 0, 2)),
        bias.reshape(1, -1),
        gain1.reshape(1, -1),
        shift1.reshape(1, -1),
    )
    centred = hidden.reshape(3, TILE, channels) - coef[0:3, None, :]
    value = centred * (coef[4:7, None, :] * gain2) + shift2
    return jax.nn.silu(value).reshape(pixels, channels)


def solution(mesh):
    return jax.shard_map(
        shards,
        mesh=mesh,
        in_specs=(
            P(("tiles", "sub"), None),
            P("tiles", None, None),
            P(),
            P(),
            P(),
            P(),
            P(),
            P(),
            P(),
        ),
        out_specs=P(("tiles", "sub"), None),
        check_vma=False,
    )
```

time: 436 us -> 71.6 us (0.16)
  blocking collectives: 309 us -> 0 us
  Pallas kernels: 0 us -> 67.5 us
  matrix products: 42.7 us -> 0 us
  local copies, waits for them, and re-layouts: 35.8 us -> 0.01 us
  starting transfers between devices: 16.8 us -> 0 us
  between operations: 14.3 us -> 0.02 us
  other arithmetic: 13.9 us -> 3.77 us
    psum x4 -> x0, blocking collectives: 309 us -> none  [the longest x2 161 us: normalize(): group_total = lax.psum(group_table(firsts), ('tiles', 'sub'))]
    pallas_call x0 -> x1, Pallas kernels: none -> 67.5 us  [shards(): pl.pallas_call(kernel, out_shape=(jax.ShapeDtypeStruct((pixels, channels)...]
    dot_general x12 -> x0, matrix products: 42.7 us -> none  [the longest x4 30 us: shards(): jnp.einsum('ktp,kto->po', taps_block, weight_block, precision=highest, pr...]
    gather x1 -> x0, local copies, waits for them, and re-layouts: 18.6 us -> none  [shards(): tapped = jnp.take(padded, all_sources, axis=1) * all_masks[None, :]]
    ppermute x2 -> x0, starting transfers between devices: 16.8 us -> none  [the longest x1 13.6 us: extended(): lax.ppermute(head, axis, [((i + 1) % count, i) for i in range(ends)])]
    dynamic_slice x1 -> x0, local copies, waits for them, and re-layouts: 9.35 us -> none  [shards(): taps_block = lax.dynamic_slice_in_dim(tapped, block_start, block_rows, 0)]
    mul x2 -> x1, other arithmetic: 12.3 us -> 2.97 us  [shards(): return jax.nn.silu(value).reshape(pixels, channels)]
    concatenate x2 -> x0, local copies, waits for them, and re-layouts: 4.49 us -> none  [the longest x1 4.48 us: extended(): jnp.concatenate([lax.ppermute(tail, axis, [(i, (i + 1) % count) for i in...]
  transfers between devices with their start and end apart: 3 -> 0, of which waited for: 0 -> 0; matrix products, arithmetic and copies ran while one was open for 13% -> 0% of each run, Pallas kernels for 0% -> 0%
where the time goes in v1:
time: 71.6 us; the launch traced here: 71.3 us
  Pallas kernels  67.5 us (94%)
  other arithmetic  3.77 us (5%)
    pallas_call x1, Pallas kernels, shards(): pl.pallas_call(kernel, out_shape=(jax.ShapeDtypeStruct((pixels, channels)...  67.5 us
    mul x1, other arithmetic, shards(): return jax.nn.silu(value).reshape(pixels, channels)  2.97 us

profile of v1, /device:TPU:1, one launch (start us, length us, event | category | flops | bytes accessed | tf_op | source)
XLA Modules:
  0.0 71.3 jit_solution(688412660958788925)
XLA Ops:
  0.0 0.0 copy-start.1
  0.0 0.0 copy-start
  0.0 67.5 %block.1 = (f32[768,512]{1,0:T(8,128)}, f32[8,512]{1,0:T(8,128)}) custom-call(s32[36]{0:T(128)} %counts.1, s32[36]{0:T(128)} %widths.1, f32[768,512]{1,0:T(8,128)} %latents.1, f32[9,16,512]{2,1,0:T(8,128)} %bitcast.16, f32[1,512]{1,0:T(1,128)} %bitcast.17, f32[1,512]{1,0:T(1,128)} %bitcast.18, f32[1,512]{1,0:T(1,128)} %bitcast.19), custom_call_target="tpu_custom_call" | custom-call | tf_op jit(solution)/shard_map/block/pallas_call | solution.py:557
  67.5 0.0 copy-done
  67.5 0.8 %fusion.1 = (f32[3,512]{1,0:T(4,128)S(1)}, f32[3,512]{1,0:T(4,128)S(1)}) fusion(f32[8,512]{1,0:T(8,128)} %get-tuple-element.8, f32[512]{0:T(512)S(1)} %copy-done), kind=kLoop, calls=%fused_computation.5 | loop fusion | flops 1536 | bytes 26624 | tf_op jit(solution)/shard_map/slice | solution.py:604
  68.3 0.0 copy-done.1
  68.3 3.0 %divide_multiply_fusion = f32[768,512]{1,0:T(8,128)} fusion(f32[768,512]{1,0:T(8,128)} %get-tuple-element.7, f32[512]{0:T(512)S(1)} %copy-done.1, f32[3,512]{1,0:T(4,128)S(1)} %get-tuple-element.10, f32[3,512]{1,0:T(4,128)S(1)} %get-tuple-element.9), kind=kLoop, calls=%fused_computation.3 | loop fusion | flops 2752512 | bytes 3160064 | tf_op jit(solution)/shard_map/jit(silu)/mul | solution.py:606
Async XLA Ops:
  0.0 68.3 %copy-start.1 = (f32[512]{0:T(512)S(1)}, f32[512]{0:T(512)}, u32[]{:S(2)}) copy-start(f32[512]{0:T(512)} %param.15) | copy-start | bytes 6148
  0.0 67.5 %copy-start = (f32[512]{0:T(512)S(1)}, f32[512]{0:T(512)}, u32[]{:S(2)}) copy-start(f32[512]{0:T(512)} %param.14) | copy-start | bytes 6148

commit v2 on v1

--- a/solution.py
+++ b/solution.py
@@ -17,9 +17,87 @@
 EPS = 1e-06
 WINDOW = 21
 PEERS = 2 * WINDOW
-A_TAPS = (0, 4)
-B_TAPS = (4, 5)
-FULL, LOW, HIGH = 0, 1, 2
+
+
+START = ([("a_start",)], [("b_start",)])
+SERVE = {
+    "stats": (
+        [("a_near", "y"), ("a_near", "a"), ("a_far", "y")],
+        [("b_z", 1, 0), ("b_z", 1, 1)],
+    ),
+    "act0": (
+        [("a_far", "a")],
+        [("b_near", 0)],
+    ),
+    "act6": (
+        [("y_near", 0, 0), ("y_near", 0, 1)],
+        [("b_z", 2, 0), ("b_z", 2, 1)],
+    ),
+    "act7": (
+        [("a_z", "y", 1, 0, 0), ("a_z", "y", 1, 1, 0)],
+        [],
+    ),
+    "pre00": (
+        [("a_z", "y", 1, 0, 1), ("a_z", "y", 1, 1, 1), ("a_done", "y", 1), ("a_done", "y", -1), ("a_z", "a", 1, 0, 0), ("a_z", "a", 1, 1, 0), ("a_z", "a", 1, 0, 1), ("a_z", "a", 1, 1, 1), ("a_done", "a", 1), ("a_done", "a", -1), ("y_far", 0), ("a_z", "y", 2, 0, 0), ("a_z", "y", 2, 1, 0), ("y_near", 1, 0), ("y_near", 1, 1), ("a_z", "y", 2, 0, 1), ("a_z", "y", 2, 1, 1), ("a_done", "y", -2), ("a_done", "y", 2), ("a_z", "a", 2, 0, 0), ("a_z", "a", 2, 1, 0), ("y_near", -1, 0), ("y_near", -1, 1), ("a_z", "a", 2, 0, 1), ("a_z", "a", 2, 1, 1), ("a_done", "a", -2), ("a_done", "a", 2), ("y_far", 1), ("a_z", "y", 3, 0, 0), ("a_z", "y", 3, 1, 0)],
+        [("b_near", -1), ("b_near", 1), ("b_far", 0), ("b_z", 3, 0), ("b_z", 3, 1), ("b_near", -2), ("b_near", 2), ("b_far", -1), ("b_far", 1), ("b_last",)],
+    ),
+    "post000": (
+        [("a_z", "y", 3, 0, 1), ("a_z", "y", 3, 1, 1), ("a_done", "y", 3), ("a_done", "y", -3), ("y_near", -2, 0), ("y_near", -2, 1)],
+        [],
+    ),
+    "post001": (
+        [("a_z", "a", 3, 0, 0), ("a_z", "a", 3, 1, 0)],
+        [("b_near", 3), ("b_near", -3)],
+    ),
+    "post002": (
+        [("a_z", "a", 3, 0, 1), ("a_z", "a", 3, 1, 1), ("a_done", "a", 3), ("a_done", "a", -3), ("y_near", 2, 0), ("y_near", 2, 1)],
+        [("b_far", -2), ("b_far", 2)],
+    ),
+    "post010": (
+        [("a_z", "y", 4, 0, 0), ("y_far", -1)],
+        [],
+    ),
+    "post011": (
+        [("a_z", "y", 4, 0, 1), ("a_done", "y", 4)],
+        [("b_near", 4)],
+    ),
+    "post012": (
+        [("a_z", "a", 4, 0, 0), ("y_near", 3, 0), ("y_near", 3, 1)],
+        [],
+    ),
+    "post100": (
+        [("a_z", "a", 4, 0, 1), ("a_done", "a", 4)],
+        [("b_far", 3), ("b_far", -3)],
+    ),
+    "post101": (
+        [("y_near", -3, 0), ("y_near", -3, 1)],
+        [],
+    ),
+    "post102": (
+        [("y_far", -2)],
+        [("b_far", 4)],
+    ),
+    "pre11": (
+        [("y_far", 2)],
+        [],
+    ),
+    "post110": (
+        [("y_near", 4, 0), ("y_near", 4, 1)],
+        [],
+    ),
+    "post111": (
+        [("y_far", 3)],
+        [],
+    ),
+    "post112": (
+        [("y_far", -3)],
+        [],
+    ),
+    "post201": (
+        [("y_far", 4)],
+        [],
+    ),
+}
 
 
 def lane_iota(shape):
@@ -124,6 +202,7 @@
     halo,
     taps_a,
     taps_b,
+    taps_y,
     acts,
     total,
     w_high,
@@ -139,17 +218,13 @@
     stat_send,
     stat_recv,
     send_sem,
-    ax_recv,
-    az_recv,
-    bz_recv,
-    bx_recv,
-    pair_recv,
+    recv_sem,
 ):
     t = lax.axis_index("tiles")
     s = lax.axis_index("sub")
     me = t * 8 + s
     z, x = t // 4, t % 4
-    core = s % 2
+    y, core = s // 2, s % 2
 
     def at(index):
         p = lax.rem(index + 256, 256)
@@ -160,6 +235,9 @@
         "z-": (lax.rem(z + 7, 8) * 4 + x, s),
         "x+": (z * 4 + lax.rem(x + 1, 4), s),
         "x-": (z * 4 + lax.rem(x + 3, 4), s),
+        "x2": (z * 4 + lax.rem(x + 2, 4), s),
+        "y+": (t, lax.rem(y + 1, 4) * 2 + core),
+        "y-": (t, lax.rem(y + 3, 4) * 2 + core),
         "c": (t, s + 1 - 2 * core),
     }
 
@@ -168,6 +246,11 @@
 
     def row_of(dz, dx):
         return z_row(dz) + lax.rem(x + dx + 4, 4)
+
+    odd = z % 2
+
+    def s_row(ds):
+        return z_row((1 - 2 * odd) * ds)
 
     barrier = pltpu.get_barrier_semaphore()
 
@@ -176,19 +259,25 @@
             pl.semaphore_signal(barrier, inc=1, device_id=at(me + sign * step), device_id_type=MESH)
         return carry
 
-    for name in ("z+", "z-", "x+", "x-"):
+    for name in ("z+", "z-", "x+", "x-", "x2", "y+", "y-"):
         pl.semaphore_signal(barrier, inc=1, device_id=right[name], device_id_type=MESH)
     lax.fori_loop(1, WINDOW + 1, greet, 0)
 
     load = pltpu.make_async_copy(latents, local, local_sem.at[0])
     load.start()
 
-    own = [
-        pltpu.make_async_copy(weight.at[pl.ds(0, 4)], taps_a.at[t], local_sem.at[1]),
-        pltpu.make_async_copy(weight.at[pl.ds(4, 5)], taps_b.at[t], local_sem.at[1]),
-    ]
-    for owner in range(2):
-        pl.when(core == owner)(own[owner].start)
+    own_a = pltpu.make_async_copy(weight.at[pl.ds(0, 1)], taps_a.at[t], local_sem.at[1])
+    own_b = pltpu.make_async_copy(weight.at[pl.ds(1, 4)], taps_b.at[t], local_sem.at[1])
+    own_y = pltpu.make_async_copy(weight.at[5 + y], taps_y.at[y, t], local_sem.at[2])
+
+    @pl.when(core == 0)
+    def _():
+        own_y.start()
+        own_a.start()
+
+    @pl.when(core == 1)
+    def _():
+        own_b.start()
 
     tiles = [3 * me + j for j in range(3)]
     starts = [me * 0] * 3
@@ -209,141 +298,176 @@
         0, counts.shape[0], place, (begin, starts, ends, width)
     )
 
-    def piece(taps, first, count):
-        if taps[0] < 4:
-            return taps_a.at[pl.ds(first, count), pl.ds(taps[0], taps[1])]
-        return taps_b.at[pl.ds(first, count), pl.ds(taps[0] - 4, taps[1])]
+    def piece(part):
+        kind, taps, first, count = part
+        if kind == "y":
+            return taps_y.at[pl.ds(taps[0], taps[1]), pl.ds(first, count)]
+        ref = taps_a if kind == "a" else taps_b
+        return ref.at[pl.ds(first, count), pl.ds(taps[0], taps[1])]
 
     sent = {0: [], 1: []}
 
-    def send(owner, taps, first, count, way, recv):
-        ref = piece(taps, first, count)
-        copy = pltpu.make_async_remote_copy(
+    def remote(part, way, send_index, recv_index):
+        ref = piece(part)
+        return pltpu.make_async_remote_copy(
             src_ref=ref,
             dst_ref=ref,
-            send_sem=send_sem.at[len(sent[owner])],
-            recv_sem=recv,
+            send_sem=send_sem.at[send_index],
+            recv_sem=recv_sem.at[recv_index],
             device_id=right[way],
             device_id_type=MESH,
         )
-        copy.start()
-        sent[owner].append((taps, count))
-
-    def arrived(taps, first, count, recv):
-        ref = piece(taps, first, count)
-        pltpu.make_async_remote_copy(
-            src_ref=ref,
-            dst_ref=ref,
-            send_sem=send_sem.at[0],
-            recv_sem=recv,
-            device_id=right["c"],
-            device_id_type=MESH,
-        ).wait_recv()
+
+    def send(owner, part, way, recv):
+        remote(part, way, len(sent[owner]), recv).start()
+        sent[owner].append((part[0], part[1][1], part[3]))
+
+    def arrived(part, recv):
+        remote(part, "c", 0, recv).wait_recv()
 
     group_of = {0: 0, -1: 1, 1: 2, -2: 3, 2: 4, -3: 5, 3: 6, 4: 7}
-    a_low, a_high = (0, 2), (2, 2)
-    b_low, b_high = (4, 2), (6, 3)
+    a_all, b_all = (0, 1), (0, 4)
+    onward = ("z+", "z-")
+
+    def a_part(kind, first, count):
+        return (kind, (y, 1) if kind == "y" else a_all, first, count)
 
     def a_start():
-        own[0].wait()
-        send(0, A_TAPS, row_of(0, 0), 1, "x+", ax_recv.at[0])
-        send(0, A_TAPS, row_of(0, 0), 1, "x-", ax_recv.at[1])
-
-    def a_x_near():
-        arrived(A_TAPS, row_of(0, -1), 1, ax_recv.at[0])
-        send(0, a_low, row_of(0, -1), 1, "x+", ax_recv.at[2])
-        arrived(A_TAPS, row_of(0, 1), 1, ax_recv.at[1])
-        send(0, a_high, row_of(0, 1), 1, "x-", ax_recv.at[3])
-
-    def a_x_far():
-        arrived(a_low, row_of(0, 2), 1, ax_recv.at[2])
-        arrived(a_high, row_of(0, 2), 1, ax_recv.at[3])
-        for h in range(2):
-            send(0, A_TAPS, z_row(0) + 2 * h, 2, "z+", az_recv.at[h])
-            send(0, A_TAPS, z_row(0) + 2 * h, 2, "z-", az_recv.at[6 + h])
-        send(0, A_TAPS, z_row(0), 4, "c", pair_recv.at[0])
-
-    def a_z(d):
-        if d == 4:
-            arrived(A_TAPS, z_row(4), 2, az_recv.at[12])
-            arrived(A_TAPS, z_row(4) + 2, 2, az_recv.at[13])
-            send(0, A_TAPS, z_row(4), 4, "c", pair_recv.at[7])
-            return
+        own_y.wait()
+        own_a.wait()
+        for k, kind in enumerate("ya"):
+            send(0, a_part(kind, row_of(0, 0), 1), "x+", 3 * k)
+            send(0, a_part(kind, row_of(0, 0), 1), "x-", 3 * k + 1)
+            send(0, a_part(kind, row_of(0, 0), 1), "x2", 3 * k + 2)
+
+    def a_near(kind):
+        k = "ya".index(kind)
+        for way in range(2):
+            arrived(a_part(kind, row_of(0, 1 if way else -1), 1), 3 * k + way)
+
+    def a_far(kind):
+        k = "ya".index(kind)
+        arrived(a_part(kind, row_of(0, 2), 1), 3 * k + 2)
         for h in range(2):
             for way in range(2):
-                dz = d if way else -d
-                row = z_row(dz) + 2 * h
-                arrived(A_TAPS, row, 2, az_recv.at[way * 6 + (d - 1) * 2 + h])
-                if d < 3:
-                    send(0, A_TAPS, row, 2, "z-" if way else "z+", az_recv.at[way * 6 + d * 2 + h])
-                elif way == h:
-                    send(0, A_TAPS, row, 2, "z-" if way else "z+", az_recv.at[12 + h])
-        for dz in (-d, d):
-            send(0, A_TAPS, z_row(dz), 4, "c", pair_recv.at[group_of[dz]])
+                part = a_part(kind, z_row(0) + 2 * h, 2)
+                send(0, part, onward[way], 6 + 14 * k + 6 * way + h)
+        a_done(kind, 0)
+
+    def a_done(kind, dz):
+        g = group_of[dz]
+        part = a_part(kind, s_row(dz), 4)
+        if kind == "y":
+            send(0, part, "y+", 34 + 4 * g)
+            send(0, part, "y-", 34 + 4 * g + 1)
+        else:
+            send(0, part, "c", 56 + g)
+
+    def a_z(kind, d, way, h):
+        k = "ya".index(kind)
+        base = 6 + 14 * k
+        if d == 4:
+            arrived(a_part(kind, z_row(4) + 2 * h, 2), base + 12 + h)
+            return
+        part = a_part(kind, z_row(d if way else -d) + 2 * h, 2)
+        arrived(part, base + 6 * way + 2 * (d - 1) + h)
+        if d < 3:
+            send(0, part, onward[way], base + 6 * way + 2 * d + h)
+        elif way == h:
+            send(0, part, onward[way], base + 12 + h)
+
+    def y_near(dz, way):
+        g = group_of[dz]
+        tap = lax.rem(y + (1 if way else 3), 4)
+        arrived(("y", (tap, 1), s_row(dz), 4), 34 + 4 * g + way)
+        send(0, ("y", (tap, 1), s_row(dz) + 2 * way, 2), "y-" if way else "y+", 34 + 4 * g + 2 + way)
+
+    def y_far(dz):
+        g = group_of[dz]
+        tap = lax.rem(y + 2, 4)
+        for way in range(2):
+            arrived(("y", (tap, 1), s_row(dz) + 2 * way, 2), 34 + 4 * g + 2 + way)
+        send(0, ("y", (0, 4), s_row(dz), 4), "c", 64 + g)
+
+    def b_halves(g):
+        return ((0, 2), (2, 2))
 
     def b_spread(dz):
         g = group_of[dz]
-        send(1, B_TAPS, row_of(dz, 0), 1, "x+", bx_recv.at[4 * g])
-        send(1, B_TAPS, row_of(dz, 0), 1, "x-", bx_recv.at[4 * g + 1])
+        if 0 < abs(dz) < 4:
+            g = 2 * dz - odd if dz > 0 else -2 * dz - 1 + odd
+        part = ("b", b_all, row_of(dz, 0), 1)
+        send(1, part, "x+", 8 + 4 * g)
+        send(1, part, "x-", 8 + 4 * g + 1)
 
     def b_start():
-        own[1].wait()
-        send(1, B_TAPS, row_of(0, 0), 1, "z+", bz_recv.at[0])
-        send(1, B_TAPS, row_of(0, 0), 1, "z-", bz_recv.at[3])
+        own_b.wait()
+        part = ("b", b_all, row_of(0, 0), 1)
+        send(1, part, "z+", 0)
+        send(1, part, "z-", 3)
         b_spread(0)
 
-    def b_z(d):
-        if d == 4:
-            arrived(b_low, row_of(4, 0), 1, bz_recv.at[6])
-            arrived(b_high, row_of(4, 0), 1, bz_recv.at[7])
-            b_spread(4)
-            return
+    def b_z(d, way):
+        dz = d if way else -d
+        part = ("b", b_all, row_of(dz, 0), 1)
+        arrived(part, 3 * way + d - 1)
+        if d < 3:
+            send(1, part, onward[way], 3 * way + d)
+        else:
+            send(1, ("b", b_halves(0)[way], row_of(dz, 0), 1), onward[way], 6 + way)
+        b_spread(dz)
+
+    def b_last():
         for way in range(2):
-            dz = d if way else -d
-            arrived(B_TAPS, row_of(dz, 0), 1, bz_recv.at[way * 3 + d - 1])
-            if d < 3:
-                send(1, B_TAPS, row_of(dz, 0), 1, "z-" if way else "z+", bz_recv.at[way * 3 + d])
-            else:
-                taps = b_high if way else b_low
-                send(1, taps, row_of(dz, 0), 1, "z-" if way else "z+", bz_recv.at[6 + way])
-            b_spread(dz)
+            arrived(("b", b_halves(0)[way], row_of(4, 0), 1), 6 + way)
+        b_spread(4)
 
     def b_near(dz):
         g = group_of[dz]
-        arrived(B_TAPS, row_of(dz, -1), 1, bx_recv.at[4 * g])
-        send(1, b_low, row_of(dz, -1), 1, "x+", bx_recv.at[4 * g + 2])
-        arrived(B_TAPS, row_of(dz, 1), 1, bx_recv.at[4 * g + 1])
-        send(1, b_high, row_of(dz, 1), 1, "x-", bx_recv.at[4 * g + 3])
+        for way in range(2):
+            first = s_row(dz) + lax.rem(x + (1 if way else 3), 4)
+            arrived(("b", b_all, first, 1), 8 + 4 * g + way)
+            send(1, ("b", b_halves(g)[way], first, 1), "x-" if way else "x+", 8 + 4 * g + 2 + way)
 
     def b_far(dz):
         g = group_of[dz]
-        arrived(b_low, row_of(dz, 2), 1, bx_recv.at[4 * g + 2])
-        arrived(b_high, row_of(dz, 2), 1, bx_recv.at[4 * g + 3])
-        send(1, B_TAPS, z_row(dz), 4, "c", pair_recv.at[g])
-
-    def serve(a_steps, b_steps):
+        for way in range(2):
+            arrived(("b", b_halves(g)[way], s_row(dz) + lax.rem(x + 2, 4), 1), 8 + 4 * g + 2 + way)
+        send(1, ("b", b_all, s_row(dz), 4), "c", 66 + g)
+
+    steps = {
+        step.__name__: step
+        for step in (
+            a_start, a_near, a_far, a_done, a_z, y_near, y_far, b_start, b_z, b_last, b_near, b_far
+        )
+    }
+
+    def serve(lists):
+        for owner in range(2):
+            if lists[owner]:
+
+                @pl.when(core == owner)
+                def _(owner=owner):
+                    for name, *values in lists[owner]:
+                        steps[name](*values)
+
+    def serve_at(slot):
+        if slot in SERVE:
+            serve(SERVE[slot])
+
+    def pair_arrived(groups, shared):
         @pl.when(core == 0)
         def _():
-            for step in a_steps:
-                step()
-
-        @pl.when(core == 1)
-        def _():
-            for step in b_steps:
-                step()
-
-    def pair_arrived(groups):
-        @pl.when(core == 0)
-        def _():
-            for dz in groups:
-                arrived(B_TAPS, z_row(dz), 4, pair_recv.at[group_of[dz]])
+            for dz in groups if shared else ():
+                arrived(("b", b_all, s_row(dz), 4), 66 + group_of[dz])
 
         @pl.when(core == 1)
         def _():
             for dz in groups:
-                arrived(A_TAPS, z_row(dz), 4, pair_recv.at[group_of[dz]])
-
-    do = functools.partial
+                if shared:
+                    arrived(("a", a_all, s_row(dz), 4), 56 + group_of[dz])
+                else:
+                    arrived(("y", (0, 4), s_row(dz), 4), 64 + group_of[dz])
 
     load.wait()
     stat1[...] = tile_stats(local)
@@ -351,8 +475,8 @@
         rows = pl.ds(96 * h, 96)
         total[rows, :] = jnp.broadcast_to(bias[...], (96, 512))
 
-    pl.semaphore_wait(barrier, PEERS + 4)
-    serve([a_start], [b_start])
+    pl.semaphore_wait(barrier, PEERS + 7)
+    serve(START)
     up = pltpu.make_async_remote_copy(
         src_ref=latents.at[pl.ds(5 * HALF, HALF), :],
         dst_ref=halo.at[0],
@@ -401,8 +525,7 @@
     share(stat1, win1, 0)
     up.start()
     down.start()
-    serve([a_x_near], [do(b_z, 1), do(b_near, 0)])
-    serve([a_x_far], [do(b_z, 2), do(b_far, 0), do(b_near, -1), do(b_near, 1)])
+    serve_at("stats")
     collect(win1, 0)
     coef[...] = image_stats(win1, stat1, me, starts, ends)
     up.wait()
@@ -438,7 +561,9 @@
                         acts[dx, 1, rows, lanes] = (low.astype(F32) * keep).astype(BF16)
 
     act_block(lambda lanes: halo[0, :, lanes], 0, width[0], [(0, tiles[0] > starts[0])])
+    serve_at("act0")
     act_block(lambda lanes: halo[1, :, lanes], 2, width[2], [(2 * 512 + 384, tiles[2] + 1 < ends[2])])
+    serve_at("act1")
     for q in range(6):
         j, half = q // 2, q % 2
         stores = [(j * 512 + HALF + half * HALF, None)]
@@ -447,13 +572,8 @@
         if half == 1 and j < 2:
             stores.append(((j + 1) * 512, tiles[j + 1] > starts[j + 1]))
         act_block(lambda lanes, q=q: local[HALF * q : HALF * (q + 1), lanes], j, width[j], stores)
-
-    serve(
-        [do(a_z, 1)],
-        [do(b_z, 3), do(b_far, -1), do(b_far, 1), do(b_near, -2), do(b_near, 2)],
-    )
-
-    odd = z % 2
+        serve_at(f"act{q + 2}")
+
     first = z // 2
     order = [
         first,
@@ -461,68 +581,62 @@
         lax.rem(first + 1 + 2 * odd, 4),
         lax.rem(first + 2, 4),
     ]
-    groups = [(0, -1, 1), (-2, 2), (-3, 3), (4,)]
-
-    def split_weights(chunk):
+    groups = [(0, 1), (-1, -2), (2, 3), (-3, 4)]
+
+    def split_weights(chunk, taps):
         def fixed(c):
-            for source, skip in ((taps_a, 0), (taps_b, 4)):
-                for tap in range(source.shape[1]):
-                    value = source[8 * c : 8 * c + 8, tap : tap + 1].reshape(HALF, 512)
-                    to = pl.ds((tap + skip) * HALF, HALF)
-                    high = value.astype(BF16)
-                    w_high[to, :] = high
-                    w_low[to, :] = (value - high.astype(F32)).astype(BF16)
+            for tap in taps:
+                if tap < 1:
+                    value = taps_a[8 * c : 8 * c + 8, tap : tap + 1]
+                elif tap < 5:
+                    value = taps_b[8 * c : 8 * c + 8, tap - 1 : tap]
+                else:
+                    value = taps_y[tap - 5 : tap - 4, 8 * c : 8 * c + 8]
+                value = value.reshape(HALF, 512)
+                to = pl.ds(tap * HALF, HALF)
+                high = value.astype(BF16)
+                w_high[to, :] = high
+                w_low[to, :] = (value - high.astype(F32)).astype(BF16)
 
         for c in range(4):
             pl.when(chunk == c)(functools.partial(fixed, c))
 
-    def multiply(chunk, j):
+    def multiply(chunk, taps, j):
         lanes = pl.ds(pl.multiple_of(chunk * HALF, HALF), HALF)
         wide = width[j]
-
         is_wide, is_middle = wide == 128, wide == 64
 
-        def taps(part):
-            columns = []
-            for dy in (-1, 0, 1):
-                for dx in range(3):
-                    base = j * 512 + HALF
-                    if dy == 0:
-                        columns.append(acts[dx, part, pl.ds(base, TILE), lanes])
-                        continue
-                    near = acts[dx, part, pl.ds(base + 32 * dy, TILE), lanes]
-                    middle = acts[dx, part, pl.ds(base + 64 * dy, TILE), lanes]
-                    far = acts[dx, part, pl.ds(base + 128 * dy, TILE), lanes]
-                    columns.append(
-                        jnp.where(is_wide, far, jnp.where(is_middle, middle, near))
-                    )
-            return jnp.concatenate(columns, axis=1)
-
-        high = taps(0)
-        low = taps(1)
-        out = jnp.dot(high, w_high[...], preferred_element_type=F32)
-        out += jnp.dot(low, w_high[...], preferred_element_type=F32)
-        out += jnp.dot(high, w_low[...], preferred_element_type=F32)
+        def columns(part):
+            blocks = []
+            for tap in taps:
+                dy, dx = tap // 3 - 1, tap % 3
+                base = j * 512 + HALF
+                if dy == 0:
+                    blocks.append(acts[dx, part, pl.ds(base, TILE), lanes])
+                    continue
+                near = acts[dx, part, pl.ds(base + 32 * dy, TILE), lanes]
+                middle = acts[dx, part, pl.ds(base + 64 * dy, TILE), lanes]
+                far = acts[dx, part, pl.ds(base + 128 * dy, TILE), lanes]
+                blocks.append(jnp.where(is_wide, far, jnp.where(is_middle, middle, near)))
+            return jnp.concatenate(blocks, axis=1)
+
+        weight_rows = pl.ds(taps[0] * HALF, len(taps) * HALF)
+        high = columns(0)
+        low = columns(1)
+        out = jnp.dot(high, w_high[weight_rows, :], preferred_element_type=F32)
+        out += jnp.dot(low, w_high[weight_rows, :], preferred_element_type=F32)
+        out += jnp.dot(high, w_low[weight_rows, :], preferred_element_type=F32)
         rows = pl.ds(pl.multiple_of(j * TILE, TILE), TILE)
         total[rows, :] += out
 
-    between = {
-        (0, 0): ([], [do(b_z, 4)]),
-        (0, 1): ([], [do(b_far, -2), do(b_far, 2)]),
-        (0, 2): ([do(a_z, 2)], [do(b_near, -3), do(b_near, 3)]),
-        (1, 0): ([], [do(b_far, -3), do(b_far, 3)]),
-        (1, 1): ([], [do(b_near, 4)]),
-        (1, 2): ([do(a_z, 3)], [do(b_far, 4)]),
-        (2, 2): ([do(a_z, 4)], []),
-    }
-
     for k in range(4):
-        pair_arrived(groups[k])
-        split_weights(order[k])
-        for j in range(3):
-            multiply(order[k], j)
-            if (k, j) in between:
-                serve(*between[(k, j)])
+        for part, taps in enumerate((range(0, 5), range(5, 9))):
+            serve_at(f"pre{k}{part}")
+            pair_arrived(groups[k], part == 0)
+            split_weights(order[k], taps)
+            for j in range(3):
+                multiply(order[k], taps, j)
+                serve_at(f"post{k}{part}{j}")
 
     store = pltpu.make_async_copy(total, hidden, local_sem.at[6])
     store.start()
@@ -532,16 +646,8 @@
 
         @pl.when(core == owner)
         def _(owner=owner):
-            for index, (taps, count) in enumerate(sent[owner]):
-                ref = piece(taps, z_row(0), count)
-                pltpu.make_async_remote_copy(
-                    src_ref=ref,
-                    dst_ref=ref,
-                    send_sem=send_sem.at[index],
-                    recv_sem=pair_recv.at[0],
-                    device_id=right["c"],
-                    device_id_type=MESH,
-                ).wait_send()
+            for index, (kind, taps, count) in enumerate(sent[owner]):
+                remote((kind, (0, taps), 0, count), "c", index, 0).wait_send()
 
     collect(win2, 1)
     coef_out[...] = image_stats(win2, stat2, me, starts, ends)
@@ -565,8 +671,9 @@
         scratch_shapes=[
             pltpu.VMEM((pixels, channels), F32),
             pltpu.VMEM((2, HALF, channels), F32),
+            pltpu.VMEM((32, 1, 16, channels), F32),
             pltpu.VMEM((32, 4, 16, channels), F32),
-            pltpu.VMEM((32, 5, 16, channels), F32),
+            pltpu.VMEM((4, 32, 16, channels), F32),
             pltpu.VMEM((3, 2, 1536, channels), BF16),
             pltpu.VMEM((pixels, channels), F32),
             pltpu.VMEM((9 * HALF, channels), BF16),
@@ -581,12 +688,8 @@
             dma((2,)),
             dma((2,)),
             dma((2,)),
-            dma((48,)),
-            dma((4,)),
-            dma((14,)),
-            dma((8,)),
-            dma((32,)),
-            dma((8,)),
+            dma((96,)),
+            dma((80,)),
         ],
         compiler_params=pltpu.CompilerParams(
             collective_id=0, has_side_effects=True, vmem_limit_bytes=60 << 20

time: 71.6 us -> 69.2 us (0.966)
  Pallas kernels: 67.5 us -> 65.2 us
    pallas_call x1, Pallas kernels: 67.5 us -> 65.2 us  [shards(): pl.pallas_call(kernel, out_shape=(jax.ShapeDtypeStruct((pixels, channels)...]
where the time goes in v2:
time: 69.2 us; the launch traced here: 69 us
  Pallas kernels  65.2 us (94%)
  other arithmetic  3.77 us (5%)
    pallas_call x1, Pallas kernels, shards(): pl.pallas_call(kernel, out_shape=(jax.ShapeDtypeStruct((pixels, channels)...  65.2 us
    mul x1, other arithmetic, shards(): return jax.nn.silu(value).reshape(pixels, channels)  2.97 us

profile of v2, /device:TPU:1, one launch (start us, length us, event | category | flops | bytes accessed | tf_op | source)
XLA Modules:
  0.0 69.0 jit_solution(16627785494206307379)
XLA Ops:
  0.0 0.0 copy-start.1
  0.0 0.0 copy-start
  0.0 65.2 %block.1 = (f32[768,512]{1,0:T(8,128)}, f32[8,512]{1,0:T(8,128)}) custom-call(s32[36]{0:T(128)} %counts.1, s32[36]{0:T(128)} %widths.1, f32[768,512]{1,0:T(8,128)} %latents.1, f32[9,16,512]{2,1,0:T(8,128)} %bitcast.16, f32[1,512]{1,0:T(1,128)} %bitcast.17, f32[1,512]{1,0:T(1,128)} %bitcast.18, f32[1,512]{1,0:T(1,128)} %bitcast.19), custom_call_target="tpu_custom_call" | custom-call | tf_op jit(solution)/shard_map/block/pallas_call | solution.py:663
  65.2 0.0 copy-done
  65.2 0.8 %fusion.1 = (f32[3,512]{1,0:T(4,128)S(1)}, f32[3,512]{1,0:T(4,128)S(1)}) fusion(f32[8,512]{1,0:T(8,128)} %get-tuple-element.8, f32[512]{0:T(512)S(1)} %copy-done), kind=kLoop, calls=%fused_computation.5 | loop fusion | flops 1536 | bytes 26624 | tf_op jit(solution)/shard_map/slice | solution.py:707
  66.0 0.0 copy-done.1
  66.0 3.0 %divide_multiply_fusion = f32[768,512]{1,0:T(8,128)} fusion(f32[768,512]{1,0:T(8,128)} %get-tuple-element.7, f32[512]{0:T(512)S(1)} %copy-done.1, f32[3,512]{1,0:T(4,128)S(1)} %get-tuple-element.10, f32[3,512]{1,0:T(4,128)S(1)} %get-tuple-element.9), kind=kLoop, calls=%fused_computation.3 | loop fusion | flops 2752512 | bytes 3160064 | tf_op jit(solution)/shard_map/jit(silu)/mul | solution.py:709
Async XLA Ops:
  0.0 66.0 %copy-start.1 = (f32[512]{0:T(512)S(1)}, f32[512]{0:T(512)}, u32[]{:S(2)}) copy-start(f32[512]{0:T(512)} %param.15) | copy-start | bytes 6148
  0.0 65.2 %copy-start = (f32[512]{0:T(512)S(1)}, f32[512]{0:T(512)}, u32[]{:S(2)}) copy-start(f32[512]{0:T(512)} %param.14) | copy-start | bytes 6148

commit v3 on v2

--- a/solution.py
+++ b/solution.py
@@ -196,8 +196,10 @@
     bias,
     gain,
     shift,
+    gain2,
     hidden,
-    coef_out,
+    mean_out,
+    scale_out,
     local,
     halo,
     taps_a,
@@ -623,9 +625,12 @@
         weight_rows = pl.ds(taps[0] * HALF, len(taps) * HALF)
         high = columns(0)
         low = columns(1)
-        out = jnp.dot(high, w_high[weight_rows, :], preferred_element_type=F32)
-        out += jnp.dot(low, w_high[weight_rows, :], preferred_element_type=F32)
-        out += jnp.dot(high, w_low[weight_rows, :], preferred_element_type=F32)
+        w1, w2 = w_high[weight_rows, :], w_low[weight_rows, :]
+        out = jnp.dot(
+            jnp.concatenate([high, low, high], axis=1),
+            jnp.concatenate([w1, w1, w2], axis=0),
+            preferred_element_type=F32,
+        )
         rows = pl.ds(pl.multiple_of(j * TILE, TILE), TILE)
         total[rows, :] += out
 
@@ -650,7 +655,9 @@
                 remote((kind, (0, taps), 0, count), "c", index, 0).wait_send()
 
     collect(win2, 1)
-    coef_out[...] = image_stats(win2, stat2, me, starts, ends)
+    final = image_stats(win2, stat2, me, starts, ends)
+    mean_out[...] = final[0:3]
+    scale_out[...] = final[4:7] * gain2[...]
     store.wait()
 
 
@@ -660,14 +667,15 @@
     hbm = pl.BlockSpec(memory_space=pl.ANY)
     dma = pltpu.SemaphoreType.DMA
     pixels, channels = latents.shape
-    hidden, coef = pl.pallas_call(
+    hidden, mean, scale = pl.pallas_call(
         kernel,
         out_shape=(
             jax.ShapeDtypeStruct((pixels, channels), F32),
-            jax.ShapeDtypeStruct((8, channels), F32),
+            jax.ShapeDtypeStruct((3, channels), F32),
+            jax.ShapeDtypeStruct((3, channels), F32),
         ),
-        in_specs=[smem, smem, hbm, hbm, vmem, vmem, vmem],
-        out_specs=(hbm, vmem),
+        in_specs=[smem, smem, hbm, hbm, vmem, vmem, vmem, vmem],
+        out_specs=(hbm, vmem, vmem),
         scratch_shapes=[
             pltpu.VMEM((pixels, channels), F32),
             pltpu.VMEM((2, HALF, channels), F32),
@@ -703,9 +711,10 @@
         bias.reshape(1, -1),
         gain1.reshape(1, -1),
         shift1.reshape(1, -1),
+        gain2.reshape(1, -1),
     )
-    centred = hidden.reshape(3, TILE, channels) - coef[0:3, None, :]
-    value = centred * (coef[4:7, None, :] * gain2) + shift2
+    centred = hidden.reshape(3, TILE, channels) - mean[:, None, :]
+    value = centred * scale[:, None, :] + shift2
     return jax.nn.silu(value).reshape(pixels, channels)
 
 

time: 69.2 us -> 68 us (0.983)
  other arithmetic: 3.77 us -> 2.99 us
    slice x1 -> x0, other arithmetic: 0.8 us -> none  [shards(): centred = hidden.reshape(3, TILE, channels) - coef[0:3, None, :]]
where the time goes in v3:
time: 68 us; the launch traced here: 67.9 us
  Pallas kernels  64.9 us (95%)
  other arithmetic  2.99 us (4%)
    pallas_call x1, Pallas kernels, shards(): pl.pallas_call(kernel, out_shape=(jax.ShapeDtypeStruct((pixels, channels)...  64.9 us
    mul x1, other arithmetic, shards(): return jax.nn.silu(value).reshape(pixels, channels)  2.99 us

profile of v3, /device:TPU:1, one launch (start us, length us, event | category | flops | bytes accessed | tf_op | source)
XLA Modules:
  0.0 67.9 jit_solution(17137408443918405885)
XLA Ops:
  0.0 0.0 copy-start
  0.0 64.9 %block.1 = (f32[768,512]{1,0:T(8,128)}, f32[3,512]{1,0:T(4,128)}, f32[3,512]{1,0:T(4,128)}) custom-call(s32[36]{0:T(128)} %counts.1, s32[36]{0:T(128)} %widths.1, f32[768,512]{1,0:T(8,128)} %latents.1, f32[9,16,512]{2,1,0:T(8,128)} %bitcast.17, f32[1,512]{1,0:T(1,128)} %bitcast.18, f32[1,512]{1,0:T(1,128)} %bitcast.19, f32[1,512]{1,0:T(1,128)} %bitcast.20, ...), custom_call_target="tpu_custom_call" | custom-call | tf_op jit(solution)/shard_map/block/pallas_call | solution.py:670
  64.9 0.0 copy-done
  64.9 3.0 %divide_multiply_fusion = f32[768,512]{1,0:T(8,128)} fusion(f32[768,512]{1,0:T(8,128)} %get-tuple-element.8, f32[512]{0:T(512)S(1)} %copy-done, f32[3,512]{1,0:T(4,128)} %get-tuple-element.10, f32[3,512]{1,0:T(4,128)} %get-tuple-element.9), kind=kLoop, calls=%fused_computation.3 | loop fusion | flops 2752512 | bytes 3160064 | tf_op jit(solution)/shard_map/jit(silu)/mul | solution.py:718
Async XLA Ops:
  0.0 64.9 %copy-start = (f32[512]{0:T(512)S(1)}, f32[512]{0:T(512)}, u32[]{:S(2)}) copy-start(f32[512]{0:T(512)} %param.15) | copy-start | bytes 6148

commit v4 on v3

--- a/solution.py
+++ b/solution.py
@@ -22,64 +22,56 @@
 START = ([("a_start",)], [("b_start",)])
 SERVE = {
     "stats": (
-        [("a_near", "y"), ("a_near", "a"), ("a_far", "y")],
+        [("a_near", "y"), ("a_near", "a")],
+        [],
+    ),
+    "act0": (
+        [("a_far", "y"), ("a_far", "a")],
         [("b_z", 1, 0), ("b_z", 1, 1)],
     ),
-    "act0": (
-        [("a_far", "a")],
+    "act1": (
+        [],
         [("b_near", 0)],
     ),
-    "act6": (
-        [("y_near", 0, 0), ("y_near", 0, 1)],
-        [("b_z", 2, 0), ("b_z", 2, 1)],
-    ),
-    "act7": (
-        [("a_z", "y", 1, 0, 0), ("a_z", "y", 1, 1, 0)],
-        [],
-    ),
     "pre00": (
-        [("a_z", "y", 1, 0, 1), ("a_z", "y", 1, 1, 1), ("a_done", "y", 1), ("a_done", "y", -1), ("a_z", "a", 1, 0, 0), ("a_z", "a", 1, 1, 0), ("a_z", "a", 1, 0, 1), ("a_z", "a", 1, 1, 1), ("a_done", "a", 1), ("a_done", "a", -1), ("y_far", 0), ("a_z", "y", 2, 0, 0), ("a_z", "y", 2, 1, 0), ("y_near", 1, 0), ("y_near", 1, 1), ("a_z", "y", 2, 0, 1), ("a_z", "y", 2, 1, 1), ("a_done", "y", -2), ("a_done", "y", 2), ("a_z", "a", 2, 0, 0), ("a_z", "a", 2, 1, 0), ("y_near", -1, 0), ("y_near", -1, 1), ("a_z", "a", 2, 0, 1), ("a_z", "a", 2, 1, 1), ("a_done", "a", -2), ("a_done", "a", 2), ("y_far", 1), ("a_z", "y", 3, 0, 0), ("a_z", "y", 3, 1, 0)],
-        [("b_near", -1), ("b_near", 1), ("b_far", 0), ("b_z", 3, 0), ("b_z", 3, 1), ("b_near", -2), ("b_near", 2), ("b_far", -1), ("b_far", 1), ("b_last",)],
+        [("y_near", 0, 0), ("y_near", 0, 1), ("a_z", "y", 1, 0, 0), ("a_z", "y", 1, 1, 0), ("a_z", "y", 1, 0, 1), ("a_z", "y", 1, 1, 1), ("a_done", "y", 1), ("a_done", "y", -1), ("a_z", "a", 1, 0, 0), ("a_z", "a", 1, 1, 0), ("a_z", "a", 1, 0, 1), ("a_z", "a", 1, 1, 1), ("a_done", "a", 1), ("a_done", "a", -1), ("y_far", 0), ("a_z", "y", 2, 0, 0), ("a_z", "y", 2, 1, 0), ("y_near", 1, 0), ("y_near", 1, 1), ("a_z", "y", 2, 0, 1), ("a_z", "y", 2, 1, 1), ("a_done", "y", -2), ("a_done", "y", 2), ("a_z", "a", 2, 0, 0), ("a_z", "a", 2, 1, 0), ("y_near", -1, 0), ("y_near", -1, 1), ("a_z", "a", 2, 0, 1), ("a_z", "a", 2, 1, 1), ("a_done", "a", -2), ("a_done", "a", 2), ("a_z", "y", 3, 0, 0), ("a_z", "y", 3, 1, 0), ("y_far", 1), ("a_z", "y", 3, 0, 1), ("a_z", "y", 3, 1, 1), ("a_done", "y", 3), ("a_done", "y", -3)],
+        [("b_z", 2, 0), ("b_z", 2, 1), ("b_near", -1), ("b_near", 1), ("b_far", 0), ("b_z", 3, 0), ("b_z", 3, 1), ("b_near", -2), ("b_near", 2), ("b_far", -1), ("b_far", 1), ("b_last",)],
     ),
     "post000": (
-        [("a_z", "y", 3, 0, 1), ("a_z", "y", 3, 1, 1), ("a_done", "y", 3), ("a_done", "y", -3), ("y_near", -2, 0), ("y_near", -2, 1)],
+        [("a_z", "a", 3, 0, 0), ("a_z", "a", 3, 1, 0)],
         [],
     ),
     "post001": (
-        [("a_z", "a", 3, 0, 0), ("a_z", "a", 3, 1, 0)],
+        [("y_near", -2, 0), ("y_near", -2, 1), ("a_z", "a", 3, 0, 1), ("a_z", "a", 3, 1, 1), ("a_done", "a", 3), ("a_done", "a", -3)],
         [("b_near", 3), ("b_near", -3)],
     ),
     "post002": (
-        [("a_z", "a", 3, 0, 1), ("a_z", "a", 3, 1, 1), ("a_done", "a", 3), ("a_done", "a", -3), ("y_near", 2, 0), ("y_near", 2, 1)],
+        [],
         [("b_far", -2), ("b_far", 2)],
     ),
     "post010": (
-        [("a_z", "y", 4, 0, 0), ("y_far", -1)],
+        [("y_near", 2, 0), ("y_near", 2, 1), ("a_z", "y", 4, 0, 0)],
         [],
     ),
     "post011": (
-        [("a_z", "y", 4, 0, 1), ("a_done", "y", 4)],
+        [("y_far", -1), ("a_z", "y", 4, 0, 1), ("a_done", "y", 4)],
         [("b_near", 4)],
     ),
     "post012": (
-        [("a_z", "a", 4, 0, 0), ("y_near", 3, 0), ("y_near", 3, 1)],
+        [("a_z", "a", 4, 0, 0)],
         [],
     ),
     "post100": (
-        [("a_z", "a", 4, 0, 1), ("a_done", "a", 4)],
+        [("y_near", 3, 0), ("y_near", 3, 1), ("a_z", "a", 4, 0, 1), ("a_done", "a", 4)],
         [("b_far", 3), ("b_far", -3)],
     ),
-    "post101": (
+    "post102": (
         [("y_near", -3, 0), ("y_near", -3, 1)],
         [],
     ),
-    "post102": (
-        [("y_far", -2)],
+    "pre11": (
+        [("y_far", -2), ("y_far", 2)],
         [("b_far", 4)],
-    ),
-    "pre11": (
-        [("y_far", 2)],
-        [],
     ),
     "post110": (
         [("y_near", 4, 0), ("y_near", 4, 1)],
@@ -93,7 +85,7 @@
         [("y_far", -3)],
         [],
     ),
-    "post201": (
+    "post202": (
         [("y_far", 4)],
         [],
     ),

time: 68 us -> 67.9 us (level)
  no operation moved by 1% of the time
where the time goes in v4:
time: 67.9 us; the launch traced here: 67.8 us
  Pallas kernels  64.7 us (95%)
  other arithmetic  2.99 us (4%)
    pallas_call x1, Pallas kernels, shards(): pl.pallas_call(kernel, out_shape=(jax.ShapeDtypeStruct((pixels, channels)...  64.7 us
    mul x1, other arithmetic, shards(): return jax.nn.silu(value).reshape(pixels, channels)  2.99 us

profile of v4, /device:TPU:1, one launch (start us, length us, event | category | flops | bytes accessed | tf_op | source)
XLA Modules:
  0.0 67.8 jit_solution(3364514800339581757)
XLA Ops:
  0.0 0.0 copy-start
  0.0 64.7 %block.1 = (f32[768,512]{1,0:T(8,128)}, f32[3,512]{1,0:T(4,128)}, f32[3,512]{1,0:T(4,128)}) custom-call(s32[36]{0:T(128)} %counts.1, s32[36]{0:T(128)} %widths.1, f32[768,512]{1,0:T(8,128)} %latents.1, f32[9,16,512]{2,1,0:T(8,128)} %bitcast.17, f32[1,512]{1,0:T(1,128)} %bitcast.18, f32[1,512]{1,0:T(1,128)} %bitcast.19, f32[1,512]{1,0:T(1,128)} %bitcast.20, ...), custom_call_target="tpu_custom_call" | custom-call | tf_op jit(solution)/shard_map/block/pallas_call | solution.py:662
  64.8 0.0 copy-done
  64.8 3.0 %divide_multiply_fusion = f32[768,512]{1,0:T(8,128)} fusion(f32[768,512]{1,0:T(8,128)} %get-tuple-element.8, f32[512]{0:T(512)S(1)} %copy-done, f32[3,512]{1,0:T(4,128)} %get-tuple-element.10, f32[3,512]{1,0:T(4,128)} %get-tuple-element.9), kind=kLoop, calls=%fused_computation.3 | loop fusion | flops 2752512 | bytes 3160064 | tf_op jit(solution)/shard_map/jit(silu)/mul | solution.py:710
Async XLA Ops:
  0.0 64.8 %copy-start = (f32[512]{0:T(512)S(1)}, f32[512]{0:T(512)}, u32[]{:S(2)}) copy-start(f32[512]{0:T(512)} %param.15) | copy-start | bytes 6148
